TPU v7x, 32 devices: a whole 2x2x4 slice. The times are simulated.
32 devices in a mesh: dp: 8 (over y, x, core), tensor: 4 (over z).
Axes of the slice: x: 2, y: 2, z: 4, core: 2. Of those that a mesh axis runs over, the one named last changes fastest.
Arguments:
- hidden_in: float32 [8192, 1536], P(('dp', 'tensor')), may hold values from -6 to 6
- cotangent: float32 [8192, 1536], P(('dp', 'tensor')), may hold values from -6 to 6
- seq_lengths: int32 [8, 4], P('dp'), may hold values from 1 to 512, 1024 in all within a row
- query_weight: bfloat16 [1536, 1536], P('dp', 'tensor'), may hold values from -0.15625 to 0.15625
- key_weight: bfloat16 [1536, 768], P('dp', 'tensor'), may hold values from -0.15625 to 0.15625
- value_weight: bfloat16 [1536, 768], P('dp', 'tensor'), may hold values from -0.15625 to 0.15625
- output_weight: bfloat16 [1536, 1536], P('tensor', 'dp'), may hold values from -1.25 to 1.25
- w_gate: bfloat16 [1536, 4096], P('dp', 'tensor'), may hold values from -0.15625 to 0.15625
- w_up: bfloat16 [1536, 4096], P('dp', 'tensor'), may hold values from -0.15625 to 0.15625
- w_down: bfloat16 [4096, 1536], P('tensor', 'dp'), may hold values from -0.09375 to 0.09375
- gain_attn: bfloat16 [1536], P('dp'), may hold values from 0.099609375 to 1.8984375
- gain_mlp: bfloat16 [1536], P('dp'), may hold values from 0.099609375 to 1.8984375
Outputs:
- block_out: float32 [8192, 1536], P(('dp', 'tensor'))
- grad_input: float32 [8192, 1536], P(('dp', 'tensor'))
- grad_query: float32 [1536, 1536], P('dp', 'tensor')
- grad_key: float32 [1536, 768], P('dp', 'tensor')
- grad_value: float32 [1536, 768], P('dp', 'tensor')
- grad_output: float32 [1536, 1536], P('tensor', 'dp')
- grad_gate: float32 [1536, 4096], P('dp', 'tensor')
- grad_upproj: float32 [1536, 4096], P('dp', 'tensor')
- grad_down: float32 [4096, 1536], P('tensor', 'dp')
- grad_attnorm: float32 [1536], P('dp')
- grad_mlpnorm: float32 [1536], P('dp')
Inputs may be any that keep to these rules, and one draw needn't show every extreme that they name: `seq_lengths`: each row's lengths sum to 1024, and the longest of each row is exactly 512.
All inputs are finite; a program needn't handle non-finite values.
Results may differ from a plain program's by a relative error of at most 0.02.
Values may be sent and summed in bfloat16 or wider, within the bound.
No kernel may reach another device: no remote copies, remote signals or barrier semaphores. Data moves between devices by JAX's collectives and lax.ppermute only.
A program may use at most 128 MiB of HBM per device.

v0:
```python
import math
import jax
import jax.numpy as jnp
from jax import lax
from jax.sharding import PartitionSpec as P

QUERY_HEADS = 16
KEY_VALUE_HEADS = 8
HEAD_SIZE = 96
EPS = 1e-05
ROPE_BASE = 100000.0


def product(formula, left_side, right_side):
    return jnp.einsum(formula, left_side, right_side, preferred_element_type=jnp.float32)


def matrix_multiply(left_side, right_side):
    return jnp.dot(left_side, right_side, preferred_element_type=jnp.float32)


def multiply_by_transpose(left_side, right_side):
    return lax.dot_general(
        left_side, right_side, (((1,), (1,)), ((), ())), preferred_element_type=jnp.float32
    )


def transposed_times(left_side, right_side):
    return lax.dot_general(
        left_side, right_side, (((0,), (0,)), ((), ())), preferred_element_type=jnp.float32
    )


def positions_of(lengths_row, length_all):
    seq_ends = jnp.cumsum(lengths_row)
    seq_starts = seq_ends - lengths_row
    token_index = jnp.arange(length_all, dtype=jnp.int32)
    segment = jnp.sum((token_index[:, None] >= seq_ends[None, :]).astype(jnp.int32), axis=1)
    chosen = segment[:, None] == jnp.arange(lengths_row.shape[0], dtype=jnp.int32)[None, :]
    offsets = jnp.sum(jnp.where(chosen, seq_starts[None, :], 0), axis=1)
    return (segment, token_index - offsets)


def rope_tables(position, head_width):
    half_width = head_width // 2
    frequency = jnp.exp(
        -(2.0 * jnp.arange(half_width, dtype=jnp.float32) / head_width)
        * jnp.log(jnp.float32(ROPE_BASE))
    )
    angles = position.astype(jnp.float32)[:, None] * frequency[None, :]
    return (jnp.cos(angles), jnp.sin(angles))


def rotate_fwd(value_tensor, cosine, sine):
    half_width = value_tensor.shape[-1] // 2
    front_half = value_tensor[..., :half_width]
    back_half = value_tensor[..., half_width:]
    return jnp.concatenate(
        [front_half * cosine - back_half * sine, back_half * cosine + front_half * sine], axis=-1
    )


def inverse_rotation(value_tensor, cosine, sine):
    half_width = value_tensor.shape[-1] // 2
    front_half = value_tensor[..., :half_width]
    back_half = value_tensor[..., half_width:]
    return jnp.concatenate(
        [front_half * cosine + back_half * sine, back_half * cosine - front_half * sine], axis=-1
    )


def norm_forward(value_tensor, gain_vector):
    inverse = lax.rsqrt(jnp.mean(value_tensor * value_tensor, axis=-1, keepdims=True) + EPS)
    unit_rows = value_tensor * inverse
    return (unit_rows, inverse, (unit_rows * gain_vector.astype(jnp.float32)).astype(jnp.bfloat16))


def norm_backward(grad_normed, unit_rows, inverse, gain_vector):
    scaled = grad_normed * gain_vector.astype(jnp.float32)
    grad_gain = jnp.sum(grad_normed * unit_rows, axis=0)
    grad_rows = inverse * (
        scaled - unit_rows * jnp.mean(scaled * unit_rows, axis=-1, keepdims=True)
    )
    return (grad_rows, grad_gain)


def block_scores(query_block, key_rows, segment_block, index_block, segment, factor):
    scores = product("qkgd,skd->kgqs", query_block, key_rows) * factor
    length_all = key_rows.shape[0]
    allowed = (segment_block[:, None] == segment[None, :]) & (
        jnp.arange(length_all, dtype=jnp.int32)[None, :] <= index_block[:, None]
    )
    return jnp.where(allowed[None, None], scores, -jnp.inf)


def attend(queries, key_rows, value_row_block, segment, block_rows):
    length_all, kv_heads, query_group_width, head_width = queries.shape
    blocks = length_all // block_rows
    factor = 1.0 / math.sqrt(head_width)
    token_index = jnp.arange(length_all, dtype=jnp.int32)

    def per_block(pieces):
        query_block, segment_block, index_block = pieces
        scores = block_scores(query_block, key_rows, segment_block, index_block, segment, factor)
        maximum = jnp.max(scores, axis=-1, keepdims=True)
        logsum = maximum + jnp.log(jnp.sum(jnp.exp(scores - maximum), axis=-1, keepdims=True))
        weights = jnp.exp(scores - logsum).astype(jnp.bfloat16)
        mixed = product("kgqs,skd->qkgd", weights, value_row_block).astype(jnp.bfloat16)
        return (mixed, logsum[..., 0])

    mixed, logsum = lax.map(
        per_block,
        (
            queries.reshape(blocks, block_rows, kv_heads, query_group_width, head_width),
            segment.reshape(blocks, block_rows),
            token_index.reshape(blocks, block_rows),
        ),
    )
    return (mixed.reshape(length_all, kv_heads, query_group_width, head_width), logsum)


def attend_back(
    queries, key_rows, value_row_block, mixed, mixed_gradient, logsum, segment, block_rows
):
    length_all, kv_heads, query_group_width, head_width = queries.shape
    blocks = length_all // block_rows
    factor = 1.0 / math.sqrt(head_width)
    token_index = jnp.arange(length_all, dtype=jnp.int32)

    def per_block(carry, pieces):
        grad_keys, grad_values = carry
        query_block, mixed_block, grad_block, logsum_block, segment_block, index_block = pieces
        scores = block_scores(query_block, key_rows, segment_block, index_block, segment, factor)
        probability = jnp.exp(scores - logsum_block[..., None])
        grad_values = grad_values + product(
            "kgqs,qkgd->skd", probability.astype(jnp.bfloat16), grad_block
        )
        grad_probs = product("qkgd,skd->kgqs", grad_block, value_row_block)
        row_delta = jnp.sum(
            grad_block.astype(jnp.float32) * mixed_block.astype(jnp.float32), axis=-1
        )
        row_delta = jnp.transpose(row_delta, (1, 2, 0))[..., None]
        grad_scores = (probability * (grad_probs - row_delta) * factor).astype(jnp.bfloat16)
        grad_query = product("kgqs,skd->qkgd", grad_scores, key_rows)
        grad_keys = grad_keys + product("kgqs,qkgd->skd", grad_scores, query_block)
        return ((grad_keys, grad_values), grad_query)

    empty_grad = jnp.zeros((length_all, kv_heads, head_width), jnp.float32)
    shape_blocks = (blocks, block_rows, kv_heads, query_group_width, head_width)
    (grad_keys, grad_values), grad_query = lax.scan(
        per_block,
        (empty_grad, empty_grad),
        (
            queries.reshape(shape_blocks),
            mixed.reshape(shape_blocks),
            mixed_gradient.reshape(shape_blocks),
            logsum,
            segment.reshape(blocks, block_rows),
            token_index.reshape(blocks, block_rows),
        ),
    )
    return (
        grad_query.reshape(length_all, kv_heads, query_group_width, head_width),
        grad_keys,
        grad_values,
    )


def local(
    hidden_in,
    cotangent,
    seq_lengths,
    query_weight,
    key_weight,
    value_weight,
    output_weight,
    w_gate,
    w_up,
    w_down,
    gain_attn,
    gain_mlp,
):
    query_group_width = QUERY_HEADS // KEY_VALUE_HEADS
    gathered = (
        lax.all_gather(query_weight, "dp", axis=0, tiled=True),
        lax.all_gather(key_weight, "dp", axis=0, tiled=True),
        lax.all_gather(value_weight, "dp", axis=0, tiled=True),
        lax.all_gather(output_weight, "dp", axis=1, tiled=True),
        lax.all_gather(w_gate, "dp", axis=0, tiled=True),
        lax.all_gather(w_up, "dp", axis=0, tiled=True),
        lax.all_gather(w_down, "dp", axis=1, tiled=True),
        lax.all_gather(gain_attn, "dp", axis=0, tiled=True),
        lax.all_gather(gain_mlp, "dp", axis=0, tiled=True),
    )
    (
        query_full,
        key_full,
        value_full,
        output_full,
        gate_full,
        up_full,
        down_full,
        gain_one,
        gain_two,
    ) = gathered
    kv_local = key_full.shape[1] // HEAD_SIZE
    unit_one, inverse_one, normed_rows_one = norm_forward(hidden_in, gain_one)
    first_normalized = lax.all_gather(normed_rows_one, "tensor", axis=0, tiled=True)
    tok_rows = first_normalized.shape[0]
    block_rows = min(512, tok_rows)
    segment, position = positions_of(seq_lengths[0], tok_rows)
    cosine, sine = rope_tables(position, HEAD_SIZE)
    cos_heads, sin_heads = (cosine[:, None, None, :], sine[:, None, None, :])
    cosine_key_table, sine_key_table = (cosine[:, None, :], sine[:, None, :])
    unrotated_queries = matrix_multiply(first_normalized, query_full).reshape(
        tok_rows, kv_local, query_group_width, HEAD_SIZE
    )
    unrotated_keys = matrix_multiply(first_normalized, key_full).reshape(
        tok_rows, kv_local, HEAD_SIZE
    )
    value_row_block = (
        matrix_multiply(first_normalized, value_full)
        .astype(jnp.bfloat16)
        .reshape(tok_rows, kv_local, HEAD_SIZE)
    )
    query_rot = rotate_fwd(unrotated_queries, cos_heads, sin_heads).astype(jnp.bfloat16)
    key_rot = rotate_fwd(unrotated_keys, cosine_key_table, sine_key_table).astype(jnp.bfloat16)
    query_rot, key_rot, value_row_block = (query_rot, key_rot, value_row_block)
    mixed, logsum = attend(query_rot, key_rot, value_row_block, segment, block_rows)
    mixed_flat = mixed.reshape(tok_rows, -1)
    residual = hidden_in + lax.psum_scatter(
        matrix_multiply(mixed_flat, output_full), "tensor", scatter_dimension=0, tiled=True
    )
    unit_two, inverse_two, normed_rows_two = norm_forward(residual, gain_two)
    normed_two = lax.all_gather(normed_rows_two, "tensor", axis=0, tiled=True)
    gate_rows = matrix_multiply(normed_two, gate_full)
    up_rows = matrix_multiply(normed_two, up_full)
    sigmoid_gate = jax.nn.sigmoid(gate_rows)
    silu_gate = gate_rows * sigmoid_gate
    project_hidden_act = (silu_gate * up_rows).astype(jnp.bfloat16)
    gate_rows, up_rows, sigmoid_gate, silu_gate, hidden_act = (
        gate_rows,
        up_rows,
        sigmoid_gate,
        silu_gate,
        project_hidden_act,
    )
    block_out = residual + lax.psum_scatter(
        matrix_multiply(hidden_act, down_full).astype(jnp.bfloat16),
        "tensor",
        scatter_dimension=0,
        tiled=True,
    ).astype(jnp.float32)
    gathered = (
        lax.all_gather(query_weight, "dp", axis=0, tiled=True),
        lax.all_gather(key_weight, "dp", axis=0, tiled=True),
        lax.all_gather(value_weight, "dp", axis=0, tiled=True),
        lax.all_gather(output_weight, "dp", axis=1, tiled=True),
        lax.all_gather(w_gate, "dp", axis=0, tiled=True),
        lax.all_gather(w_up, "dp", axis=0, tiled=True),
        lax.all_gather(w_down, "dp", axis=1, tiled=True),
        lax.all_gather(gain_attn, "dp", axis=0, tiled=True),
        lax.all_gather(gain_mlp, "dp", axis=0, tiled=True),
    )
    (
        query_full,
        key_full,
        value_full,
        output_full,
        gate_full,
        up_full,
        down_full,
        gain_one,
        gain_two,
    ) = gathered
    cot_low = lax.all_gather(cotangent.astype(jnp.bfloat16), "tensor", axis=0, tiled=True)
    grad_act = multiply_by_transpose(cot_low, down_full)
    grad_down = transposed_times(hidden_act, cot_low)
    grad_gate_rows = (
        grad_act * up_rows * sigmoid_gate * (1.0 + gate_rows * (1.0 - sigmoid_gate))
    ).astype(jnp.bfloat16)
    grad_up_rows = (grad_act * silu_gate).astype(jnp.bfloat16)
    grad_gate = transposed_times(normed_two, grad_gate_rows)
    grad_upproj = transposed_times(normed_two, grad_up_rows)
    grad_normed_two = lax.psum_scatter(
        (
            multiply_by_transpose(grad_gate_rows, gate_full)
            + multiply_by_transpose(grad_up_rows, up_full)
        ).astype(jnp.bfloat16),
        "tensor",
        scatter_dimension=0,
        tiled=True,
    ).astype(jnp.float32)
    grad_middle, grad_gain_two = norm_backward(grad_normed_two, unit_two, inverse_two, gain_two)
    grad_resid = cotangent + grad_middle
    narrow_gradient = lax.all_gather(grad_resid.astype(jnp.bfloat16), "tensor", axis=0, tiled=True)
    grad_output = transposed_times(mixed_flat, narrow_gradient)
    mixed_gradient = (
        multiply_by_transpose(narrow_gradient, output_full)
        .astype(jnp.bfloat16)
        .reshape(tok_rows, kv_local, query_group_width, HEAD_SIZE)
    )
    grad_qrot, rotated_key_gradient, gradient_values_list = attend_back(
        query_rot, key_rot, value_row_block, mixed, mixed_gradient, logsum, segment, block_rows
    )
    grad_q = (
        inverse_rotation(grad_qrot, cos_heads, sin_heads).astype(jnp.bfloat16).reshape(tok_rows, -1)
    )
    key_gradient = (
        inverse_rotation(rotated_key_gradient, cosine_key_table, sine_key_table)
        .astype(jnp.bfloat16)
        .reshape(tok_rows, -1)
    )
    value_gradient = gradient_values_list.astype(jnp.bfloat16).reshape(tok_rows, -1)
    grad_query = transposed_times(first_normalized, grad_q)
    grad_key = transposed_times(first_normalized, key_gradient)
    grad_value = transposed_times(first_normalized, value_gradient)
    grad_normed_one = lax.psum_scatter(
        (
            multiply_by_transpose(grad_q, query_full)
            + multiply_by_transpose(key_gradient, key_full)
            + multiply_by_transpose(value_gradient, value_full)
        ).astype(jnp.bfloat16),
        "tensor",
        scatter_dimension=0,
        tiled=True,
    ).astype(jnp.float32)
    grad_first, grad_gain_one = norm_backward(grad_normed_one, unit_one, inverse_one, gain_one)
    grad_input = grad_resid + grad_first
    summed = (
        lax.psum_scatter(
            grad_query.astype(jnp.bfloat16), "dp", scatter_dimension=0, tiled=True
        ).astype(jnp.float32),
        lax.psum_scatter(
            grad_key.astype(jnp.bfloat16), "dp", scatter_dimension=0, tiled=True
        ).astype(jnp.float32),
        lax.psum_scatter(
            grad_value.astype(jnp.bfloat16), "dp", scatter_dimension=0, tiled=True
        ).astype(jnp.float32),
        lax.psum_scatter(
            grad_output.astype(jnp.bfloat16), "dp", scatter_dimension=1, tiled=True
        ).astype(jnp.float32),
        lax.psum_scatter(
            grad_gate.astype(jnp.bfloat16), "dp", scatter_dimension=0, tiled=True
        ).astype(jnp.float32),
        lax.psum_scatter(
            grad_upproj.astype(jnp.bfloat16), "dp", scatter_dimension=0, tiled=True
        ).astype(jnp.float32),
        lax.psum_scatter(
            grad_down.astype(jnp.bfloat16), "dp", scatter_dimension=1, tiled=True
        ).astype(jnp.float32),
        lax.psum_scatter(
            grad_gain_one.astype(jnp.bfloat16), "dp", scatter_dimension=0, tiled=True
        ).astype(jnp.float32),
        lax.psum_scatter(
            grad_gain_two.astype(jnp.bfloat16), "dp", scatter_dimension=0, tiled=True
        ).astype(jnp.float32),
    )
    output_grad = summed[3]
    gain_totals = lax.psum((summed[7], summed[8]), "tensor")
    return (
        block_out,
        grad_input,
        summed[0],
        summed[1],
        summed[2],
        output_grad,
        summed[4],
        summed[5],
        summed[6],
        gain_totals[0],
        gain_totals[1],
    )


def solution(mesh):
    in_specs = (
        P(("dp", "tensor"), None),
        P(("dp", "tensor"), None),
        P("dp", None),
        P("dp", "tensor"),
        P("dp", "tensor"),
        P("dp", "tensor"),
        P("tensor", "dp"),
        P("dp", "tensor"),
        P("dp", "tensor"),
        P("tensor", "dp"),
        P("dp"),
        P("dp"),
    )
    out_specs = (
        P(("dp", "tensor"), None),
        P(("dp", "tensor"), None),
        P("dp", "tensor"),
        P("dp", "tensor"),
        P("dp", "tensor"),
        P("tensor", "dp"),
        P("dp", "tensor"),
        P("dp", "tensor"),
        P("tensor", "dp"),
        P("dp"),
        P("dp"),
    )
    return jax.shard_map(local, mesh=mesh, in_specs=in_specs, out_specs=out_specs, check_vma=False)
```

profile of v0, /device:TPU:0, one launch (start us, length us, event | category | flops | bytes accessed | tf_op | source)
XLA Modules:
  0.0 1093.3 jit_solution(17131380025793593165)
XLA Ops:
  12.6 16.0 %all-reduce.6 = (bf16[1536]{0:T(1024)(128)(2,1)S(1)}, bf16[1536]{0:T(1024)(128)(2,1)}) all-reduce(bf16[1536]{0:T(1024)(128)(2,1)S(1)} %dynamic-update-slice, bf16[1536]{0:T(1024)(128)(2,1)S(1)} %dynamic-update-slice.1), channel_id=1, replica_groups=mesh['dp'=8,'tensor'=4] {'dp'}, use_global_device_ids=true, to_apply=%add | all-reduce | flops 3072 | bytes 12288
  28.7 2.5 multiply_convert_fusion.4
  33.8 10.5 all_gather.51
  44.3 11.2 %all_gather.52 = bf16[1536,192]{1,0:T(8,128)(2,1)} all-gather(bf16[192,192]{1,0:T(8,128)(2,1)S(1)} %copy-done.27), channel_id=1, replica_groups=mesh['dp'=8,'tensor'=4] {'dp'}, dimensions={0}, use_global_device_ids=true | all-gather | bytes 663552 | tf_op jit(solution)/shard_map/all_gather | solution.py:187
  56.3 37.9 %all-gather.10.cloned.1.call-done = bf16[1024,1536]{1,0:T(8,128)(2,1)} async-done(((bf16[256,1536]{1,0:T(8,128)(2,1)}), bf16[1024,1536]{1,0:T(8,128)(2,1)}) %all-gather.10.cloned.1.call-update) | async-done | bytes 3145744 | tf_op jit(solution)/shard_map/all_gather | solution.py:208
  94.2 3.4 fusion.77
  98.4 20.2 %all-gather.12.cloned.1.call-done = bf16[1536,384]{1,0:T(8,128)(2,1)} async-done(((bf16[192,384]{1,0:T(8,128)(2,1)}), bf16[1536,384]{1,0:T(8,128)(2,1)}) %all-gather.12.cloned.1.call-update) | async-done | bytes 1179664 | tf_op jit(solution)/shard_map/all_gather | solution.py:185
  118.6 2.7 fusion.76
  130.9 22.1 %while.27 = (s32[]{:T(128)}, bf16[2,512,2,2,96]{1,4,3,2,0:T(8,128)(2,1)}, f32[2,2,2,512]{3,2,1,0:T(2,128)}, s32[2,512]{1,0:T(2,128)}, s32[1024]{0:T(1024)S(1)}, ...) while((s32[]{:T(128)}, ...), condition=%wide.region_7.8_spmd, body=%wide.region_4.7_spmd.sunk | while | flops 830142464 | bytes 28917884 | solution.py:111
  132.5 2.7 bitcast_reduce_fusion.2
  135.1 2.4 fusion.152
  138.1 4.0 fusion.153
  143.4 2.7 bitcast_reduce_fusion.2
  146.1 2.4 fusion.152
  149.0 4.0 fusion.153
  155.1 6.1 fusion.78
  161.9 110.3 %reduce-scatter.12.cloned.1.call-done = f32[256,1536]{1,0:T(8,128)} async-done(((f32[1024,1536]{1,0:T(8,128)}), f32[256,1536]{1,0:T(8,128)}) %reduce-scatter.12.cloned.1.call-update) | async-done | bytes 1572880 | tf_op jit(solution)/shard_map/reduce_scatter | solution.py:231
  279.2 27.5 %all-gather.20.cloned.1.call-done = bf16[1536,1024]{1,0:T(8,128)(2,1)} async-done(((bf16[192,1024]{1,0:T(8,128)(2,1)}), bf16[1536,1024]{1,0:T(8,128)(2,1)}) %all-gather.20.cloned.1.call-update) | async-done | bytes 3145744 | tf_op jit(solution)/shard_map/all_gather | solution.py:190
  306.6 65.5 %all-gather.16.cloned.1.call-done = bf16[1024,1536]{1,0:T(8,128)(2,1)} async-done(((bf16[256,1536]{1,0:T(8,128)(2,1)}), bf16[1024,1536]{1,0:T(8,128)(2,1)}) %all-gather.16.cloned.1.call-update) | async-done | bytes 3145744 | tf_op jit(solution)/shard_map/all_gather | solution.py:235
  372.1 8.3 fusion.80
  380.4 24.5 %all-gather.18.cloned.1.call-done = bf16[1536,1024]{1,0:T(8,128)(2,1)} async-done(((bf16[192,1024]{1,0:T(8,128)(2,1)}), bf16[1536,1024]{1,0:T(8,128)(2,1)}) %all-gather.18.cloned.1.call-update) | async-done | bytes 3145744 | tf_op jit(solution)/shard_map/all_gather | solution.py:189
  404.9 8.2 fusion.79
  413.1 57.4 %all-gather.24.cloned.1.call-done = bf16[1024,1536]{1,0:T(8,128)(2,1)} async-done(((bf16[256,1536]{1,0:T(8,128)(2,1)}), bf16[1024,1536]{1,0:T(8,128)(2,1)}) %all-gather.24.cloned.1.call-update) | async-done | bytes 3145744 | tf_op jit(solution)/shard_map/all_gather | solution.py:276
  470.5 32.7 %all-gather.22.cloned.1.call-done = bf16[1024,1536]{0,1:T(8,128)(2,1)} async-done(((bf16[1024,192]{0,1:T(8,128)(2,1)}), bf16[1024,1536]{0,1:T(8,128)(2,1)}) %all-gather.22.cloned.1.call-update) | async-done | bytes 3145744 | tf_op jit(solution)/shard_map/all_gather | solution.py:191
  503.2 11.6 %multiply_convert_fusion = (bf16[1024,1024]{1,0:T(8,128)(2,1)S(1)}, bf16[1024,1024]{1,0:T(8,128)(2,1)S(1)}, bf16[1024,1024]{1,0:T(8,128)(2,1)}) fusion(f32[1024,1024]{1,0:T(8,128)} %fusion.79, f32[1024,1024]{1,0:T(8,128)} %fusion.80, bf16[1024,1536]{1,0:T(8,128)(2,1)} %all-gather.24.cloned.1.call-done, bf16[1024,1536]{0,1:T(8,128)(2,1)} %all-gather.22.cloned.1.call-done), kind=kOutput, calls=%fused_computation.68 | convolution fusion | flops 3236954112 | bytes 20971520 | tf_op jit(solution)/shard_map/dot_general | solution.py:23
  514.8 3.5 fusion.81
  518.3 5.1 add_convert_fusion.1
  523.5 60.5 %reduce-scatter.16.cloned.1.call-done = bf16[256,1536]{1,0:T(8,128)(2,1)} async-done(((bf16[1024,1536]{1,0:T(8,128)(2,1)}), bf16[256,1536]{1,0:T(8,128)(2,1)}) %reduce-scatter.16.cloned.1.call-update) | async-done | bytes 786448 | tf_op jit(solution)/shard_map/reduce_scatter | solution.py:285
  584.0 2.3 fusion.71
  586.9 2.4 fusion.74
  589.4 7.6 convolution_convert_fusion
  597.1 8.0 convolution_convert_fusion.1
  605.2 7.7 convolution_convert_fusion.2
  613.0 39.9 %all-gather.26.cloned.1.call-done = bf16[1024,1536]{1,0:T(8,128)(2,1)} async-done(((bf16[256,1536]{1,0:T(8,128)(2,1)}), bf16[1024,1536]{1,0:T(8,128)(2,1)}) %all-gather.26.cloned.1.call-update) | async-done | bytes 3145744 | tf_op jit(solution)/shard_map/all_gather | solution.py:296
  652.9 4.6 convolution_convert_fusion.8
  657.5 4.6 reshape.374
  662.1 2.4 copy.40
  664.5 68.3 %while.28 = (s32[]{:T(128)}, f32[1024,2,96]{0,2,1:T(8,128)}, f32[1024,2,96]{0,2,1:T(8,128)}, f32[2,512,2,2,96]{1,0,4,3,2:T(2,128)}, bf16[2,512,2,2,96]{1,4,3,2,0...) while((s32[]{:T(128)}, f32[1024,2,96]{0,2,1:T(8,128)}, ...), condition=%wide.region_15.16_spmd.clone, body=%wide.region_13.15_spmd.clone.sunk | while | flops 2039478272 | bytes 50004156 | solution.py:150
  667.6 2.3 fusion.164
  669.9 3.4 fusion.169
  673.4 4.5 fusion.167
  677.9 2.7 fusion.168
  682.9 15.0 %dynamic_update_slice.20 = f32[2,512,2,2,96]{1,0,4,3,2:T(2,128)} dynamic-update-slice(f32[2,512,2,2,96]{1,0,4,3,2:T(2,128)} %get-tuple-element.535, f32[1,512,2,2,96]{1,0,4,3,2:T(1,128)S(1)} %copy.60, s32[]{:T(128)S(6)} %copy.79, s32[]{:T(128)} %constant.62.clone.1..sunk, s32[]{:T(128)} %constant.62.clone.1..sunk, s32[]{:T(128)} %constant.62.clone.1..sunk, s32[]{:T(128)} %constant.62.clone.1..sunk) | dynamic-update-slice | bytes 1572868 | tf_op jit(solution)/shard_map/while/body/jit(dynamic_update_index_in_dim)/dynamic_update_slice | solution.py:150
  703.4 4.6 fusion.169
  707.9 4.5 fusion.167
  712.4 3.1 fusion.168
  717.8 15.0 %dynamic_update_slice.20 = f32[2,512,2,2,96]{1,0,4,3,2:T(2,128)} dynamic-update-slice(f32[2,512,2,2,96]{1,0,4,3,2:T(2,128)} %get-tuple-element.535, f32[1,512,2,2,96]{1,0,4,3,2:T(1,128)S(1)} %copy.60, s32[]{:T(128)S(6)} %copy.79, s32[]{:T(128)} %constant.62.clone.1..sunk, s32[]{:T(128)} %constant.62.clone.1..sunk, s32[]{:T(128)} %constant.62.clone.1..sunk, s32[]{:T(128)} %constant.62.clone.1..sunk) | dynamic-update-slice | bytes 1572868 | tf_op jit(solution)/shard_map/while/body/jit(dynamic_update_index_in_dim)/dynamic_update_slice | solution.py:150
  734.8 3.9 convolution_convert_fusion.6
  741.3 4.2 convolution_convert_fusion.7
  745.5 4.7 convolution_convert_fusion.4
  750.3 2.6 reshape.354
  754.9 2.9 convolution_convert_fusion.5
  761.1 2.7 add_convert_fusion
  764.1 8.0 convolution_convert_fusion.3
  776.9 22.8 %reduce-scatter.28.cloned.1.call-done = bf16[192,1024]{1,0:T(8,128)(2,1)} async-done(((bf16[1536,1024]{1,0:T(8,128)(2,1)}), bf16[192,1024]{1,0:T(8,128)(2,1)}) %reduce-scatter.28.cloned.1.call-update) | async-done | bytes 393232 | tf_op jit(solution)/shard_map/reduce_scatter | solution.py:343
  801.6 36.0 %reduce-scatter.24.cloned.1.call-done = bf16[192,192]{1,0:T(8,128)(2,1)} async-done(((bf16[1536,192]{1,0:T(8,128)(2,1)}), bf16[192,192]{1,0:T(8,128)(2,1)}) %reduce-scatter.24.cloned.1.call-update) | async-done | bytes 73744 | tf_op jit(solution)/shard_map/reduce_scatter | solution.py:337
  839.2 36.4 %reduce-scatter.22.cloned.1.call-done = bf16[192,192]{1,0:T(8,128)(2,1)} async-done(((bf16[1536,192]{1,0:T(8,128)(2,1)}), bf16[192,192]{1,0:T(8,128)(2,1)}) %reduce-scatter.22.cloned.1.call-update) | async-done | bytes 73744 | tf_op jit(solution)/shard_map/reduce_scatter | solution.py:334
  877.2 38.8 %reduce-scatter.26.cloned.1.call-done = bf16[384,192]{0,1:T(8,128)(2,1)} async-done(((bf16[384,1536]{0,1:T(8,128)(2,1)}), bf16[384,192]{0,1:T(8,128)(2,1)}) %reduce-scatter.26.cloned.1.call-update) | async-done | bytes 147472 | tf_op jit(solution)/shard_map/reduce_scatter | solution.py:340
  917.6 38.7 %reduce-scatter.20.cloned.1.call-done = bf16[192,384]{1,0:T(8,128)(2,1)} async-done(((bf16[1536,384]{1,0:T(8,128)(2,1)}), bf16[192,384]{1,0:T(8,128)(2,1)}) %reduce-scatter.20.cloned.1.call-update) | async-done | bytes 147472 | tf_op jit(solution)/shard_map/reduce_scatter | solution.py:331
  958.0 61.1 %reduce-scatter.18.cloned.1.call-done = bf16[256,1536]{1,0:T(8,128)(2,1)} async-done(((bf16[1024,1536]{1,0:T(8,128)(2,1)}), bf16[256,1536]{1,0:T(8,128)(2,1)}) %reduce-scatter.18.cloned.1.call-update) | async-done | bytes 786448 | tf_op jit(solution)/shard_map/reduce_scatter | solution.py:318
  1020.8 13.5 %all-reduce.5 = (bf16[1536]{0:T(1024)(128)(2,1)S(1)}, bf16[1536]{0:T(1024)(128)(2,1)S(1)}) all-reduce(bf16[1536]{0:T(1024)(128)(2,1)S(1)} %get-tuple-element.256, bf16[1536]{0:T(1024)(128)(2,1)S(1)} %copy-done.32), channel_id=13, replica_groups=mesh['dp'=8,'tensor'=4] {'dp'}, use_global_device_ids=true, to_apply=%region_26.27.clone | all-reduce | flops 3072 | bytes 12288
  1034.4 12.1 %all-reduce.4 = (f32[192]{0:T(256)}, f32[192]{0:T(256)}) all-reduce(f32[192]{0:T(256)S(1)} %get-tuple-element.336, f32[192]{0:T(256)S(1)} %get-tuple-element.335), channel_id=1, replica_groups=mesh['dp'=8,'tensor'=4] {'tensor'}, use_global_device_ids=true, to_apply=%region_27.28 | all-reduce | flops 384 | bytes 3072 | tf_op jit(solution)/shard_map/psum | solution.py:360
  1046.5 35.3 %reduce-scatter.14.cloned.1.call-done = bf16[256,1536]{1,0:T(8,128)(2,1)} async-done(((bf16[1024,1536]{1,0:T(8,128)(2,1)}), bf16[256,1536]{1,0:T(8,128)(2,1)}) %reduce-scatter.14.cloned.1.call-update) | async-done | bytes 786448 | tf_op jit(solution)/shard_map/reduce_scatter | solution.py:248
  1081.8 4.5 fusion.67
  (199 shorter events, 69.9 us)
Async XLA Ops:
  7.2 25.6 %copy-start.38 = (s32[1,4]{1,0:T(1,128)S(1)}, s32[1,4]{1,0:T(1,128)}, u32[]{:S(2)}) copy-start(s32[1,4]{1,0:T(1,128)} %param.18) | copy-start | bytes 52
  7.2 26.6 %copy-start.26 = (bf16[192,192]{1,0:T(8,128)(2,1)S(1)}, bf16[192,192]{1,0:T(8,128)(2,1)}, u32[]{:S(2)}) copy-start(bf16[192,192]{1,0:T(8,128)(2,1)} %param.20) | copy-start | bytes 221188
  7.2 37.1 %copy-start.27 = (bf16[192,192]{1,0:T(8,128)(2,1)S(1)}, bf16[192,192]{1,0:T(8,128)(2,1)}, u32[]{:S(2)}) copy-start(bf16[192,192]{1,0:T(8,128)(2,1)} %param.21) | copy-start | bytes 221188
  7.2 87.0 %all-gather.10.cloned.1.call-start = ((), (), s32[]{:S(2)}) async-start(), calls=%async_computation.11 | async-start | bytes 3932160 | tf_op jit(solution)/shard_map/all_gather | solution.py:208
  8.9 35.3 %copy-start.30 = (f32[256]{0:T(256)}, f32[256]{0:T(256)S(1)}, u32[]{:S(2)}) copy-start(f32[256]{0:T(256)S(1)} %add_rsqrt_fusion.1) | copy-start | bytes 3076
  28.7 15.6 %copy-start.24 = (f32[1536]{0:T(1024)}, f32[1536]{0:T(1024)S(1)}, u32[]{:S(2)}) copy-start(f32[1536]{0:T(1024)S(1)} %convert_element_type.158) | copy-start | bytes 18436
  31.2 87.4 %all-gather.12.cloned.1.call-start = ((), (), s32[]{:S(2)}) async-start(), calls=%async_computation.12 | async-start | bytes 1327104 | tf_op jit(solution)/shard_map/all_gather | solution.py:185
  31.9 123.2 %all-gather.14.cloned.1.call-start = ((), (), s32[]{:S(2)}) async-start(), calls=%async_computation.13 | async-start | bytes 1327104 | tf_op jit(solution)/shard_map/all_gather | solution.py:188
  32.7 239.5 %reduce-scatter.12.cloned.1.call-start = ((), (), s32[]{:S(2)}) async-start(), calls=%async_computation.14 | async-start | bytes 7864320 | tf_op jit(solution)/shard_map/reduce_scatter | solution.py:231
  56.3 65.1 %copy-start.10 = (f32[1024,48]{0,1:T(8,128)}, f32[1024,48]{0,1:T(8,128)S(1)}, u32[]{:S(2)}) copy-start(f32[1024,48]{0,1:T(8,128)S(1)} %get-tuple-element.331) | copy-start | bytes 589828
  56.3 65.1 %copy-start.12 = (f32[1024,48]{0,1:T(8,128)}, f32[1024,48]{0,1:T(8,128)S(1)}, u32[]{:S(2)}) copy-start(f32[1024,48]{0,1:T(8,128)S(1)} %get-tuple-element.332) | copy-start | bytes 589828
  94.2 24.5 %copy-start.5 = (bf16[1024,1536]{1,0:T(8,128)(2,1)S(1)}, bf16[1024,1536]{1,0:T(8,128)(2,1)}, u32[]{:S(2)}) copy-start(bf16[1024,1536]{1,0:T(8,128)(2,1)} %all-gather.10.cloned.1.call-done) | copy-start | bytes 9437188
  125.8 3.1 copy-start.22
  125.8 3.1 copy-start.23
  125.8 3.1 copy-start.7
  155.1 6.1 copy-start.14
  161.2 0.7 copy-start.35
  161.2 111.0 %copy-start = (f32[256,1536]{1,0:T(8,128)S(1)}, f32[256,1536]{1,0:T(8,128)}, u32[]{:S(2)}) copy-start(f32[256,1536]{1,0:T(8,128)} %param.16) | copy-start | bytes 4718596
  161.2 145.4 %all-gather.20.cloned.1.call-start = ((), (), s32[]{:S(2)}) async-start(), calls=%async_computation.17 | async-start | bytes 3538944 | tf_op jit(solution)/shard_map/all_gather | solution.py:190
  161.8 210.3 %all-gather.16.cloned.1.call-start = ((), (), s32[]{:S(2)}) async-start(), calls=%async_computation.15 | async-start | bytes 3932160 | tf_op jit(solution)/shard_map/all_gather | solution.py:235
  161.9 115.0 %copy-start.4 = (f32[256,1536]{1,0:T(8,128)S(1)}, f32[256,1536]{1,0:T(8,128)}, u32[]{:S(2)}) copy-start(f32[256,1536]{1,0:T(8,128)} %param.17) | copy-start | bytes 4718596
  273.8 1.1 copy-start.2
  273.9 1.1 copy-start.28
  276.1 128.8 %all-gather.18.cloned.1.call-start = ((), (), s32[]{:S(2)}) async-start(), calls=%async_computation.16 | async-start | bytes 3538944 | tf_op jit(solution)/shard_map/all_gather | solution.py:189
  276.8 193.6 %all-gather.24.cloned.1.call-start = ((), (), s32[]{:S(2)}) async-start(), calls=%async_computation.20 | async-start | bytes 3932160 | tf_op jit(solution)/shard_map/all_gather | solution.py:276
  277.9 225.3 %all-gather.22.cloned.1.call-start = ((), (), s32[]{:S(2)}) async-start(), calls=%async_computation.18 | async-start | bytes 3538944 | tf_op jit(solution)/shard_map/all_gather | solution.py:191
  278.6 305.4 %reduce-scatter.16.cloned.1.call-start = ((), (), s32[]{:S(2)}) async-start(), calls=%async_computation.21 | async-start | bytes 3932160 | tf_op jit(solution)/shard_map/reduce_scatter | solution.py:285
  503.2 11.6 %copy-start.37 = (bf16[1536,1024]{1,0:T(8,128)(2,1)S(1)}, bf16[1536,1024]{1,0:T(8,128)(2,1)}, u32[]{:S(2)}) copy-start(bf16[1536,1024]{1,0:T(8,128)(2,1)} %all-gather.18.cloned.1.call-done) | copy-start | bytes 9437188
  514.8 3.5 copy-start.39
  514.8 3.5 copy-start.40
  514.8 3.5 copy-start.36
  523.4 60.6 %copy-start.3 = (f32[256,1536]{1,0:T(8,128)S(1)}, f32[256,1536]{1,0:T(8,128)}, u32[]{:S(2)}) copy-start(f32[256,1536]{1,0:T(8,128)} %copy-done.2) | copy-start | bytes 4718596
  523.4 129.4 %all-gather.26.cloned.1.call-start = ((), (), s32[]{:S(2)}) async-start(), calls=%async_computation.22 | async-start | bytes 3932160 | tf_op jit(solution)/shard_map/all_gather | solution.py:296
  586.3 0.6 copy-start.33
  589.4 183.5 %reduce-scatter.32.cloned.1.call-start = ((), (), s32[]{:S(2)}) async-start(), calls=%async_computation.30 | async-start | bytes 3538944 | tf_op jit(solution)/shard_map/reduce_scatter | solution.py:349
  597.1 177.8 %reduce-scatter.30.cloned.1.call-start = ((), (), s32[]{:S(2)}) async-start(), calls=%async_computation.29 | async-start | bytes 3538944 | tf_op jit(solution)/shard_map/reduce_scatter | solution.py:346
  605.1 194.5 %reduce-scatter.28.cloned.1.call-start = ((), (), s32[]{:S(2)}) async-start(), calls=%async_computation.28 | async-start | bytes 3538944 | tf_op jit(solution)/shard_map/reduce_scatter | solution.py:343
  612.9 40.0 %copy-start.21 = (bf16[384,1536]{0,1:T(8,128)(2,1)S(1)}, bf16[384,1536]{0,1:T(8,128)(2,1)}, u32[]{:S(2)}) copy-start(bf16[384,1536]{0,1:T(8,128)(2,1)} %all-gather.14.cloned.1.call-done) | copy-start | bytes 3538948
  612.9 224.7 %reduce-scatter.24.cloned.1.call-start = ((), (), s32[]{:S(2)}) async-start(), calls=%async_computation.26 | async-start | bytes 884736 | tf_op jit(solution)/shard_map/reduce_scatter | solution.py:337
  734.0 0.7 copy-start.18
  734.8 4.4 copy-start.11
  734.8 4.4 copy-start.13
  738.8 136.9 %reduce-scatter.22.cloned.1.call-start = ((), (), s32[]{:S(2)}) async-start(), calls=%async_computation.25 | async-start | bytes 884736 | tf_op jit(solution)/shard_map/reduce_scatter | solution.py:334
  740.5 0.7 copy-start.16
  741.3 4.2 copy-start.15
  745.5 170.5 %reduce-scatter.26.cloned.1.call-start = ((), (), s32[]{:S(2)}) async-start(), calls=%async_computation.27 | async-start | bytes 1327104 | tf_op jit(solution)/shard_map/reduce_scatter | solution.py:340
  750.3 206.0 %reduce-scatter.20.cloned.1.call-start = ((), (), s32[]{:S(2)}) async-start(), calls=%async_computation.24 | async-start | bytes 1327104 | tf_op jit(solution)/shard_map/reduce_scatter | solution.py:331
  753.0 1.9 copy-start.6
  754.9 2.9 copy-start.9
  754.9 2.9 copy-start.17
  757.8 261.3 %reduce-scatter.18.cloned.1.call-start = ((), (), s32[]{:S(2)}) async-start(), calls=%async_computation.23 | async-start | bytes 3932160 | tf_op jit(solution)/shard_map/reduce_scatter | solution.py:318
  757.8 1.4 copy-start.20
  759.2 1.9 copy-start.8
  759.2 1.9 copy-start.19
  763.9 317.9 %reduce-scatter.14.cloned.1.call-start = ((), (), s32[]{:S(2)}) async-start(), calls=%async_computation.19 | async-start | bytes 3932160 | tf_op jit(solution)/shard_map/reduce_scatter | solution.py:248
  772.1 246.9 %copy-start.1 = (f32[256,1536]{1,0:T(8,128)S(1)}, f32[256,1536]{1,0:T(8,128)}, u32[]{:S(2)}) copy-start(f32[256,1536]{1,0:T(8,128)} %param.16) | copy-start | bytes 4718596
  772.1 246.9 %copy-start.25 = (f32[1536]{0:T(1024)S(1)}, f32[1536]{0:T(1024)}, u32[]{:S(2)}) copy-start(f32[1536]{0:T(1024)} %copy-done.24) | copy-start | bytes 18436
  772.1 246.9 %copy-start.31 = (f32[256]{0:T(256)S(1)}, f32[256]{0:T(256)}, u32[]{:S(2)}) copy-start(f32[256]{0:T(256)} %copy-done.30) | copy-start | bytes 3076
  774.9 245.9 %copy-start.32 = (bf16[1536]{0:T(1024)(128)(2,1)S(1)}, bf16[1536]{0:T(1024)(128)(2,1)}, u32[]{:S(2)}) copy-start(bf16[1536]{0:T(1024)(128)(2,1)} %get-tuple-element.254) | copy-start | bytes 9220
  774.9 306.9 %copy-start.29 = (f32[256]{0:T(256)S(1)}, f32[256]{0:T(256)}, u32[]{:S(2)}) copy-start(f32[256]{0:T(256)} %copy-done.28) | copy-start | bytes 3076
  774.9 306.9 %copy-start.34 = (f32[256]{0:T(256)S(1)}, f32[256]{0:T(256)}, u32[]{:S(2)}) copy-start(f32[256]{0:T(256)} %copy-done.33) | copy-start | bytes 3076
Sparse Core Ops, SparseCore 0:
  31.3 62.7 all-gather.9
  96.0 22.5 all-gather.11
  120.5 23.9 all-gather.13
  161.4 110.7 reduce-scatter.11
  273.9 32.6 all-gather.19
  308.6 63.4 all-gather.15
  374.0 30.8 all-gather.17
  407.0 63.4 all-gather.23
  472.4 30.8 all-gather.21
  523.6 60.3 reduce-scatter.15
  589.5 63.3 all-gather.25
  656.1 44.6 reduce-scatter.31
  704.2 46.0 reduce-scatter.29
  753.6 46.0 reduce-scatter.27
  802.7 34.9 reduce-scatter.23
  840.6 34.9 reduce-scatter.21
  879.3 36.6 reduce-scatter.25
  919.6 36.6 reduce-scatter.19
  958.6 60.3 reduce-scatter.17
  1021.2 60.5 reduce-scatter.13
where the time goes:
time: 1100 us; the launch traced here: 1090 us
  waiting for transfers between devices  749 us (68%)
  matrix products  152 us (14%)
  blocking collectives  63.4 us (6%)
  local copies, waits for them, and re-layouts  60.7 us (6%)
  other arithmetic  49.9 us (5%)
  between operations  16.5 us (2%)
    reduce_scatter x1, waiting for transfers between devices, local(): lax.psum_scatter(matrix_multiply(mixed_flat, output_full), 'tensor', scat...  110 us
    all_gather x1, waiting for transfers between devices, local(): normed_two = lax.all_gather(normed_rows_two, 'tensor', axis=0, tiled=True)  65.5 us
    reduce_scatter x1, waiting for transfers between devices, local(): lax.psum_scatter((multiply_by_transpose(grad_q, query_full) + multiply_by...  61.1 us
    reduce_scatter x1, waiting for transfers between devices, local(): lax.psum_scatter((multiply_by_transpose(grad_gate_rows, gate_full) + mult...  60.5 us
    all_gather x1, waiting for transfers between devices, local(): lax.all_gather(cotangent.astype(jnp.bfloat16), 'tensor', axis=0, tiled=True)  57.4 us
    dot_general x14, matrix products, product(): jnp.einsum(formula, left_side, right_side, preferred_element_type=jnp.flo...  43.7 us
    all_gather x1, waiting for transfers between devices, local(): lax.all_gather(grad_resid.astype(jnp.bfloat16), 'tensor', axis=0, tiled=T...  39.9 us
    dot_general x7, matrix products, transposed_times(): lax.dot_general(left_side, right_side, (((0,), (0,)), ((), ())), preferre...  39 us
  transfers between devices with their start and end apart: 20, of which 17 were waited for; matrix products, arithmetic and copies ran while one was open for 20% of the time, Pallas kernels for 0%

commit v1 on v0

--- a/solution.py
+++ b/solution.py
@@ -232,7 +232,14 @@
         matrix_multiply(mixed_flat, output_full), "tensor", scatter_dimension=0, tiled=True
     )
     unit_two, inverse_two, normed_rows_two = norm_forward(residual, gain_two)
-    normed_two = lax.all_gather(normed_rows_two, "tensor", axis=0, tiled=True)
+    size = lax.axis_size("tensor")
+    hops = [(i, (i + 1) % size) for i in range(size)]
+    parts = [normed_rows_two]
+    for hop in range(1, size):
+        parts = [lax.ppermute(parts[0], "tensor", hops), *parts]
+    whole = jnp.concatenate(parts, axis=0)
+    shift = (lax.axis_index("tensor") + 1) * parts[-1].shape[0]
+    normed_two = jnp.roll(whole, shift, axis=0)
     gate_rows = matrix_multiply(normed_two, gate_full)
     up_rows = matrix_multiply(normed_two, up_full)
     sigmoid_gate = jax.nn.sigmoid(gate_rows)

time: 1100 us -> 1060 us (0.964)
  waiting for transfers between devices: 749 us -> 677 us
  starting transfers between devices: 1.92 us -> 27.9 us
    all_gather x1 -> x0, waiting for transfers between devices: 65.5 us -> none  [local(): normed_two = lax.all_gather(normed_rows_two, 'tensor', axis=0, tiled=True)]
    ppermute x0 -> x3, waiting for transfers between devices: none -> 61.6 us  [local(): parts = [lax.ppermute(parts[0], 'tensor', hops), *parts]]
    all_gather x1, waiting for transfers between devices: 57.4 us -> 0.83 us  [local(): lax.all_gather(cotangent.astype(jnp.bfloat16), 'tensor', axis=0, tiled=True)]
    ppermute x0 -> x3, starting transfers between devices: none -> 26.5 us  [local(): parts = [lax.ppermute(parts[0], 'tensor', hops), *parts]]
    all_gather x1, waiting for transfers between devices: 27.5 us -> 15.7 us  [local(): lax.all_gather(w_up, 'dp', axis=0, tiled=True)]
  transfers between devices with their start and end apart: 20 -> 22, of which waited for: 17 -> 18; matrix products, arithmetic and copies ran while one was open for 20% -> 21% of each run, Pallas kernels for 0% -> 0%
where the time goes in v1:
time: 1060 us; the launch traced here: 1050 us
  waiting for transfers between devices  677 us (64%)
  matrix products  150 us (14%)
  local copies, waits for them, and re-layouts  67.3 us (6%)
  blocking collectives  61.4 us (6%)
  other arithmetic  49.3 us (5%)
  starting transfers between devices  27.9 us (3%)
  between operations  16.2 us (2%)
    reduce_scatter x1, waiting for transfers between devices, local(): lax.psum_scatter(matrix_multiply(mixed_flat, output_full), 'tensor', scat...  106 us
    ppermute x3, waiting for transfers between devices, local(): parts = [lax.ppermute(parts[0], 'tensor', hops), *parts]  61.6 us
    reduce_scatter x1, waiting for transfers between devices, local(): lax.psum_scatter((multiply_by_transpose(grad_q, query_full) + multiply_by...  61 us
    reduce_scatter x1, waiting for transfers between devices, local(): lax.psum_scatter((multiply_by_transpose(grad_gate_rows, gate_full) + mult...  60.5 us
    dot_general x7, matrix products, matrix_multiply(): return jnp.dot(left_side, right_side, preferred_element_type=jnp.float32)  44.5 us
    dot_general x14, matrix products, product(): jnp.einsum(formula, left_side, right_side, preferred_element_type=jnp.flo...  39.9 us
    all_gather x1, waiting for transfers between devices, local(): lax.all_gather(grad_resid.astype(jnp.bfloat16), 'tensor', axis=0, tiled=T...  39.8 us
    all_gather x1, waiting for transfers between devices, local(): lax.all_gather(normed_rows_one, 'tensor', axis=0, tiled=True)  39.8 us
  transfers between devices with their start and end apart: 22, of which 18 were waited for; matrix products, arithmetic and copies ran while one was open for 21% of the time, Pallas kernels for 0%

profile of v1, /device:TPU:0, one launch (start us, length us, event | category | flops | bytes accessed | tf_op | source)
XLA Modules:
  0.0 1049.8 jit_solution(16941948533028186055)
XLA Ops:
  12.7 16.0 %all-reduce.6 = (bf16[1536]{0:T(1024)(128)(2,1)S(1)}, bf16[1536]{0:T(1024)(128)(2,1)}) all-reduce(bf16[1536]{0:T(1024)(128)(2,1)S(1)} %dynamic-update-slice, bf16[1536]{0:T(1024)(128)(2,1)S(1)} %dynamic-update-slice.1), channel_id=1, replica_groups=mesh['dp'=8,'tensor'=4] {'dp'}, use_global_device_ids=true, to_apply=%add | all-reduce | flops 3072 | bytes 12288
  28.7 2.5 multiply_convert_fusion.4
  33.8 9.4 all_gather.48
  43.2 10.4 all_gather.49
  54.4 39.8 %all-gather.9.cloned.1.call-done = bf16[1024,1536]{1,0:T(8,128)(2,1)} async-done(((bf16[256,1536]{1,0:T(8,128)(2,1)}), bf16[1024,1536]{1,0:T(8,128)(2,1)}) %all-gather.9.cloned.1.call-update) | async-done | bytes 3145744 | tf_op jit(solution)/shard_map/all_gather | solution.py:208
  94.2 3.1 fusion.87
  97.4 21.3 %all-gather.11.cloned.1.call-done = bf16[1536,384]{1,0:T(8,128)(2,1)} async-done(((bf16[192,384]{1,0:T(8,128)(2,1)}), bf16[1536,384]{1,0:T(8,128)(2,1)}) %all-gather.11.cloned.1.call-update) | async-done | bytes 1179664 | tf_op jit(solution)/shard_map/all_gather | solution.py:185
  118.7 3.6 fusion.86
  124.3 3.8 convolution_convert_fusion.9
  128.2 20.1 %while.27 = (s32[]{:T(128)}, bf16[2,512,2,2,96]{1,4,3,2,0:T(8,128)(2,1)}, f32[2,2,2,512]{3,2,1,0:T(2,128)}, s32[2,512]{1,0:T(2,128)}, s32[1024]{0:T(1024)S(1)}, ...) while((s32[]{:T(128)}, ...), condition=%wide.region_7.8_spmd, body=%wide.region_4.7_spmd.sunk | while | flops 830142464 | bytes 28917884 | solution.py:111
  131.4 2.3 fusion.157
  134.4 4.0 fusion.158
  141.3 2.3 fusion.157
  144.3 4.0 fusion.158
  148.3 2.2 copy.37
  150.7 6.0 fusion.88
  161.2 106.5 %reduce-scatter.12.cloned.1.call-done = f32[256,1536]{1,0:T(8,128)} async-done(((f32[1024,1536]{1,0:T(8,128)}), f32[256,1536]{1,0:T(8,128)}) %reduce-scatter.12.cloned.1.call-update) | async-done | bytes 1572880 | tf_op jit(solution)/shard_map/reduce_scatter | solution.py:231
  271.7 29.2 %collective-permute-done = bf16[256,1536]{1,0:T(8,128)(2,1)S(1)} collective-permute-done((bf16[256,1536]{1,0:T(8,128)(2,1)S(1)}, bf16[256,1536]{1,0:T(8,128)(2,1)S(1)}, u32[]{:S(2)}, u32[]{:S(2)}) %collective-permute-start) | collective-permute-done | bytes 786464 | tf_op jit(solution)/shard_map/ppermute | solution.py:239
  300.9 11.7 %collective-permute-start.1 = (bf16[256,1536]{1,0:T(8,128)(2,1)S(1)}, bf16[256,1536]{1,0:T(8,128)(2,1)S(1)}, u32[]{:S(2)}, u32[]{:S(2)}) collective-permute-start(bf16[256,1536]{1,0:T(8,128)(2,1)S(1)} %collective-permute-done), channel_id=1, source_target_pairs={{0,1},{1,2},{2,3},{3,0},{4,5},{5,6},{6,7},{7,4},{8,9},{9,10},{10,1... | collective-permute-start | bytes 2359304 | tf_op jit(solution)/shard_map/ppermute | solution.py:239
  312.7 32.4 %collective-permute-done.1 = bf16[256,1536]{1,0:T(8,128)(2,1)S(1)} collective-permute-done((bf16[256,1536]{1,0:T(8,128)(2,1)S(1)}, bf16[256,1536]{1,0:T(8,128)(2,1)S(1)}, u32[]{:S(2)}, u32[]{:S(2)}) %collective-permute-start.1) | collective-permute-done | bytes 786464 | tf_op jit(solution)/shard_map/ppermute | solution.py:239
  345.1 13.2 %collective-permute-start.2 = (bf16[256,1536]{1,0:T(8,128)(2,1)S(1)}, bf16[256,1536]{1,0:T(8,128)(2,1)}, u32[]{:S(2)}, u32[]{:S(2)}) collective-permute-start(bf16[256,1536]{1,0:T(8,128)(2,1)S(1)} %collective-permute-done.1), channel_id=1, source_target_pairs={{0,1},{1,2},{2,3},{3,0},{4,5},{5,6},{6,7},{7,4},{8,9},{9,10},{10,1... | collective-permute-start | bytes 2359304 | tf_op jit(solution)/shard_map/ppermute | solution.py:239
  359.2 32.2 %all-gather.19.cloned.1.call-done = bf16[1024,1536]{0,1:T(8,128)(2,1)} async-done(((bf16[1024,192]{0,1:T(8,128)(2,1)}), bf16[1024,1536]{0,1:T(8,128)(2,1)}) %all-gather.19.cloned.1.call-update) | async-done | bytes 3145744 | tf_op jit(solution)/shard_map/all_gather | solution.py:191
  391.3 8.2 fusion.89
  409.8 15.7 %all-gather.17.cloned.1.call-done = bf16[1536,1024]{1,0:T(8,128)(2,1)} async-done(((bf16[192,1024]{1,0:T(8,128)(2,1)}), bf16[1536,1024]{1,0:T(8,128)(2,1)}) %all-gather.17.cloned.1.call-update) | async-done | bytes 3145744 | tf_op jit(solution)/shard_map/all_gather | solution.py:190
  425.4 8.2 fusion.63
  433.6 25.9 %all-gather.15.cloned.1.call-done = bf16[1536,1024]{1,0:T(8,128)(2,1)} async-done(((bf16[192,1024]{1,0:T(8,128)(2,1)}), bf16[1536,1024]{1,0:T(8,128)(2,1)}) %all-gather.15.cloned.1.call-update) | async-done | bytes 3145744 | tf_op jit(solution)/shard_map/all_gather | solution.py:189
  459.5 11.7 %multiply_convert_fusion = (bf16[1024,1024]{1,0:T(8,128)(2,1)S(1)}, bf16[1024,1024]{1,0:T(8,128)(2,1)S(1)}, bf16[1024,1024]{1,0:T(8,128)(2,1)}) fusion(f32[1024,1024]{1,0:T(8,128)} %fusion.89, f32[1024,1024]{1,0:T(8,128)} %fusion.63, bf16[1536,1024]{1,0:T(8,128)(2,1)} %all-gather.15.cloned.1.call-done, ...), kind=kOutput, calls=%fused_computation.68 | convolution fusion | flops 3236954112 | bytes 20971524 | tf_op jit(solution)/shard_map/dot_general | solution.py:19
  471.3 3.5 fusion.90
  474.8 5.1 add_convert_fusion.1
  480.0 60.5 %reduce-scatter.16.cloned.1.call-done = bf16[256,1536]{1,0:T(8,128)(2,1)} async-done(((bf16[1024,1536]{1,0:T(8,128)(2,1)}), bf16[256,1536]{1,0:T(8,128)(2,1)}) %reduce-scatter.16.cloned.1.call-update) | async-done | bytes 786448 | tf_op jit(solution)/shard_map/reduce_scatter | solution.py:292
  540.5 2.3 fusion.77
  543.4 2.4 fusion.84
  545.9 7.7 convolution_convert_fusion
  553.7 8.0 convolution_convert_fusion.1
  561.8 7.7 convolution_convert_fusion.2
  569.5 39.8 %all-gather.23.cloned.1.call-done = bf16[1024,1536]{1,0:T(8,128)(2,1)} async-done(((bf16[256,1536]{1,0:T(8,128)(2,1)}), bf16[1024,1536]{1,0:T(8,128)(2,1)}) %all-gather.23.cloned.1.call-update) | async-done | bytes 3145744 | tf_op jit(solution)/shard_map/all_gather | solution.py:303
  609.4 4.6 convolution_convert_fusion.8
  613.9 4.6 reshape.374
  618.6 3.6 copy.40
  622.2 66.8 %while.28 = (s32[]{:T(128)}, f32[1024,2,96]{0,2,1:T(8,128)}, f32[1024,2,96]{0,2,1:T(8,128)}, f32[2,512,2,2,96]{1,0,4,3,2:T(2,128)}, bf16[2,512,2,2,96]{1,4,3,2,0...) while((s32[]{:T(128)}, f32[1024,2,96]{0,2,1:T(8,128)}, ...), condition=%wide.region_15.16_spmd.clone, body=%wide.region_13.15_spmd.clone.sunk | while | flops 2039478272 | bytes 50004156 | solution.py:150
  626.8 4.4 fusion.174
  631.2 4.6 fusion.172
  639.8 15.0 %dynamic_update_slice.20 = f32[2,512,2,2,96]{1,0,4,3,2:T(2,128)} dynamic-update-slice(f32[2,512,2,2,96]{1,0,4,3,2:T(2,128)} %get-tuple-element.535, f32[1,512,2,2,96]{1,0,4,3,2:T(1,128)S(1)} %copy.60, s32[]{:T(128)S(6)} %copy.86, s32[]{:T(128)} %constant.85.clone.1..sunk, s32[]{:T(128)} %constant.85.clone.1..sunk, s32[]{:T(128)} %constant.85.clone.1..sunk, s32[]{:T(128)} %constant.85.clone.1..sunk) | dynamic-update-slice | bytes 1572868 | tf_op jit(solution)/shard_map/while/body/jit(dynamic_update_index_in_dim)/dynamic_update_slice | solution.py:150
  659.4 4.7 fusion.174
  664.1 4.6 fusion.172
  668.7 3.0 fusion.173
  673.9 15.1 %dynamic_update_slice.20 = f32[2,512,2,2,96]{1,0,4,3,2:T(2,128)} dynamic-update-slice(f32[2,512,2,2,96]{1,0,4,3,2:T(2,128)} %get-tuple-element.535, f32[1,512,2,2,96]{1,0,4,3,2:T(1,128)S(1)} %copy.60, s32[]{:T(128)S(6)} %copy.86, s32[]{:T(128)} %constant.85.clone.1..sunk, s32[]{:T(128)} %constant.85.clone.1..sunk, s32[]{:T(128)} %constant.85.clone.1..sunk, s32[]{:T(128)} %constant.85.clone.1..sunk) | dynamic-update-slice | bytes 1572868 | tf_op jit(solution)/shard_map/while/body/jit(dynamic_update_index_in_dim)/dynamic_update_slice | solution.py:150
  690.9 3.9 convolution_convert_fusion.6
  697.4 3.9 convolution_convert_fusion.7
  701.3 4.7 convolution_convert_fusion.4
  706.2 2.7 reshape.354
  710.7 2.9 convolution_convert_fusion.5
  716.8 2.8 add_convert_fusion
  719.9 8.0 convolution_convert_fusion.3
  732.7 23.6 %reduce-scatter.28.cloned.1.call-done = bf16[192,1024]{1,0:T(8,128)(2,1)} async-done(((bf16[1536,1024]{1,0:T(8,128)(2,1)}), bf16[192,1024]{1,0:T(8,128)(2,1)}) %reduce-scatter.28.cloned.1.call-update) | async-done | bytes 393232 | tf_op jit(solution)/shard_map/reduce_scatter | solution.py:350
  758.3 36.0 %reduce-scatter.24.cloned.1.call-done = bf16[192,192]{1,0:T(8,128)(2,1)} async-done(((bf16[1536,192]{1,0:T(8,128)(2,1)}), bf16[192,192]{1,0:T(8,128)(2,1)}) %reduce-scatter.24.cloned.1.call-update) | async-done | bytes 73744 | tf_op jit(solution)/shard_map/reduce_scatter | solution.py:344
  795.9 36.4 %reduce-scatter.22.cloned.1.call-done = bf16[192,192]{1,0:T(8,128)(2,1)} async-done(((bf16[1536,192]{1,0:T(8,128)(2,1)}), bf16[192,192]{1,0:T(8,128)(2,1)}) %reduce-scatter.22.cloned.1.call-update) | async-done | bytes 73744 | tf_op jit(solution)/shard_map/reduce_scatter | solution.py:341
  833.9 38.8 %reduce-scatter.26.cloned.1.call-done = bf16[384,192]{0,1:T(8,128)(2,1)} async-done(((bf16[384,1536]{0,1:T(8,128)(2,1)}), bf16[384,192]{0,1:T(8,128)(2,1)}) %reduce-scatter.26.cloned.1.call-update) | async-done | bytes 147472 | tf_op jit(solution)/shard_map/reduce_scatter | solution.py:347
  874.3 38.7 %reduce-scatter.20.cloned.1.call-done = bf16[192,384]{1,0:T(8,128)(2,1)} async-done(((bf16[1536,384]{1,0:T(8,128)(2,1)}), bf16[192,384]{1,0:T(8,128)(2,1)}) %reduce-scatter.20.cloned.1.call-update) | async-done | bytes 147472 | tf_op jit(solution)/shard_map/reduce_scatter | solution.py:338
  914.7 61.0 %reduce-scatter.18.cloned.1.call-done = bf16[256,1536]{1,0:T(8,128)(2,1)} async-done(((bf16[1024,1536]{1,0:T(8,128)(2,1)}), bf16[256,1536]{1,0:T(8,128)(2,1)}) %reduce-scatter.18.cloned.1.call-update) | async-done | bytes 786448 | tf_op jit(solution)/shard_map/reduce_scatter | solution.py:325
  977.4 13.5 %all-reduce.5 = (bf16[1536]{0:T(1024)(128)(2,1)S(1)}, bf16[1536]{0:T(1024)(128)(2,1)S(1)}) all-reduce(bf16[1536]{0:T(1024)(128)(2,1)S(1)} %get-tuple-element.256, bf16[1536]{0:T(1024)(128)(2,1)S(1)} %copy-done.32), channel_id=13, replica_groups=mesh['dp'=8,'tensor'=4] {'dp'}, use_global_device_ids=true, to_apply=%region_26.27.clone | all-reduce | flops 3072 | bytes 12288
  991.0 12.0 %all-reduce.4 = (f32[192]{0:T(256)}, f32[192]{0:T(256)}) all-reduce(f32[192]{0:T(256)S(1)} %get-tuple-element.336, f32[192]{0:T(256)S(1)} %get-tuple-element.335), channel_id=1, replica_groups=mesh['dp'=8,'tensor'=4] {'tensor'}, use_global_device_ids=true, to_apply=%region_27.28 | all-reduce | flops 384 | bytes 3072 | tf_op jit(solution)/shard_map/psum | solution.py:367
  1003.0 35.5 %reduce-scatter.14.cloned.1.call-done = bf16[256,1536]{1,0:T(8,128)(2,1)} async-done(((bf16[1024,1536]{1,0:T(8,128)(2,1)}), bf16[256,1536]{1,0:T(8,128)(2,1)}) %reduce-scatter.14.cloned.1.call-update) | async-done | bytes 786448 | tf_op jit(solution)/shard_map/reduce_scatter | solution.py:255
  1038.6 4.5 fusion.73
  (208 shorter events, 77.1 us)
Async XLA Ops:
  7.2 25.6 %copy-start.37 = (s32[1,4]{1,0:T(1,128)S(1)}, s32[1,4]{1,0:T(1,128)}, u32[]{:S(2)}) copy-start(s32[1,4]{1,0:T(1,128)} %param.18) | copy-start | bytes 52
  7.2 26.6 %copy-start.25 = (bf16[192,192]{1,0:T(8,128)(2,1)S(1)}, bf16[192,192]{1,0:T(8,128)(2,1)}, u32[]{:S(2)}) copy-start(bf16[192,192]{1,0:T(8,128)(2,1)} %param.20) | copy-start | bytes 221188
  7.2 36.0 %copy-start.26 = (bf16[192,192]{1,0:T(8,128)(2,1)S(1)}, bf16[192,192]{1,0:T(8,128)(2,1)}, u32[]{:S(2)}) copy-start(bf16[192,192]{1,0:T(8,128)(2,1)} %param.21) | copy-start | bytes 221188
  7.2 87.0 %all-gather.9.cloned.1.call-start = ((), (), s32[]{:S(2)}) async-start(), calls=%async_computation.11 | async-start | bytes 3932160 | tf_op jit(solution)/shard_map/all_gather | solution.py:208
  8.9 34.3 %copy-start.30 = (f32[256]{0:T(256)}, f32[256]{0:T(256)S(1)}, u32[]{:S(2)}) copy-start(f32[256]{0:T(256)S(1)} %add_rsqrt_fusion.1) | copy-start | bytes 3076
  28.7 5.1 copy-start.23
  31.2 87.4 %all-gather.11.cloned.1.call-start = ((), (), s32[]{:S(2)}) async-start(), calls=%async_computation.12 | async-start | bytes 1327104 | tf_op jit(solution)/shard_map/all_gather | solution.py:185
  32.0 118.7 %all-gather.13.cloned.1.call-start = ((), (), s32[]{:S(2)}) async-start(), calls=%async_computation.13 | async-start | bytes 1327104 | tf_op jit(solution)/shard_map/all_gather | solution.py:188
  32.7 234.9 %reduce-scatter.12.cloned.1.call-start = ((), (), s32[]{:S(2)}) async-start(), calls=%async_computation.14 | async-start | bytes 7864320 | tf_op jit(solution)/shard_map/reduce_scatter | solution.py:231
  43.2 54.2 %copy-start.9 = (bf16[1536,192]{1,0:T(8,128)(2,1)}, bf16[1536,192]{1,0:T(8,128)(2,1)S(1)}, u32[]{:S(2)}) copy-start(bf16[1536,192]{1,0:T(8,128)(2,1)S(1)} %all_gather.48) | copy-start | bytes 1769476
  53.6 70.7 %copy-start.7 = (bf16[1536,192]{1,0:T(8,128)(2,1)}, bf16[1536,192]{1,0:T(8,128)(2,1)S(1)}, u32[]{:S(2)}) copy-start(bf16[1536,192]{1,0:T(8,128)(2,1)S(1)} %all_gather.49) | copy-start | bytes 1769476
  54.4 68.0 %copy-start.11 = (f32[1024,48]{0,1:T(8,128)}, f32[1024,48]{0,1:T(8,128)S(1)}, u32[]{:S(2)}) copy-start(f32[1024,48]{0,1:T(8,128)S(1)} %get-tuple-element.331) | copy-start | bytes 589828
  54.4 68.0 %copy-start.13 = (f32[1024,48]{0,1:T(8,128)}, f32[1024,48]{0,1:T(8,128)S(1)}, u32[]{:S(2)}) copy-start(f32[1024,48]{0,1:T(8,128)S(1)} %get-tuple-element.332) | copy-start | bytes 589828
  148.3 8.4 copy-start.2
  150.7 6.0 copy-start.15
  156.7 1.4 copy-start.4
  156.7 110.9 %copy-start = (f32[256,1536]{1,0:T(8,128)S(1)}, f32[256,1536]{1,0:T(8,128)}, u32[]{:S(2)}) copy-start(f32[256,1536]{1,0:T(8,128)} %param.16) | copy-start | bytes 4718596
  156.8 202.4 %all-gather.21.cloned.1.call-start = ((), (), s32[]{:S(2)}) async-start(), calls=%async_computation.19 | async-start | bytes 3932160 | tf_op jit(solution)/shard_map/all_gather | solution.py:283
  159.1 232.2 %all-gather.19.cloned.1.call-start = ((), (), s32[]{:S(2)}) async-start(), calls=%async_computation.17 | async-start | bytes 3538944 | tf_op jit(solution)/shard_map/all_gather | solution.py:191
  159.7 265.8 %all-gather.17.cloned.1.call-start = ((), (), s32[]{:S(2)}) async-start(), calls=%async_computation.16 | async-start | bytes 3538944 | tf_op jit(solution)/shard_map/all_gather | solution.py:190
  160.4 299.1 %all-gather.15.cloned.1.call-start = ((), (), s32[]{:S(2)}) async-start(), calls=%async_computation.15 | async-start | bytes 3538944 | tf_op jit(solution)/shard_map/all_gather | solution.py:189
  269.3 0.6 copy-start.27
  270.1 30.8 %collective-permute-start = (bf16[256,1536]{1,0:T(8,128)(2,1)S(1)}, bf16[256,1536]{1,0:T(8,128)(2,1)S(1)}, u32[]{:S(2)}, u32[]{:S(2)}) collective-permute-start(bf16[256,1536]{1,0:T(8,128)(2,1)S(1)} %multiply_convert_fusion.3), channel_id=1, source_target_pairs={{0,1},{1,2},{2,3},{3,0},{4,5},{5,6},{6,7},{7,4},{8,9},{9,10},{10,1... | collective-permute-start | bytes 2359304 | tf_op jit(solution)/shard_map/ppermute | solution.py:239
  271.7 268.8 %reduce-scatter.16.cloned.1.call-start = ((), (), s32[]{:S(2)}) async-start(), calls=%async_computation.20 | async-start | bytes 3932160 | tf_op jit(solution)/shard_map/reduce_scatter | solution.py:292
  300.9 44.2 %collective-permute-start.1 = (bf16[256,1536]{1,0:T(8,128)(2,1)S(1)}, bf16[256,1536]{1,0:T(8,128)(2,1)S(1)}, u32[]{:S(2)}, u32[]{:S(2)}) collective-permute-start(bf16[256,1536]{1,0:T(8,128)(2,1)S(1)} %collective-permute-done), channel_id=1, source_target_pairs={{0,1},{1,2},{2,3},{3,0},{4,5},{5,6},{6,7},{7,4},{8,9},{9,10},{10,1... | collective-permute-start | bytes 2359304 | tf_op jit(solution)/shard_map/ppermute | solution.py:239
  345.1 54.5 %collective-permute-start.2 = (bf16[256,1536]{1,0:T(8,128)(2,1)S(1)}, bf16[256,1536]{1,0:T(8,128)(2,1)}, u32[]{:S(2)}, u32[]{:S(2)}) collective-permute-start(bf16[256,1536]{1,0:T(8,128)(2,1)S(1)} %collective-permute-done.1), channel_id=1, source_target_pairs={{0,1},{1,2},{2,3},{3,0},{4,5},{5,6},{6,7},{7,4},{8,9},{9,10},{10,1... | collective-permute-start | bytes 2359304 | tf_op jit(solution)/shard_map/ppermute | solution.py:239
  399.6 4.0 copy-start.28
  459.5 11.7 %copy-start.36 = (bf16[1536,1024]{1,0:T(8,128)(2,1)S(1)}, bf16[1536,1024]{1,0:T(8,128)(2,1)}, u32[]{:S(2)}) copy-start(bf16[1536,1024]{1,0:T(8,128)(2,1)} %all-gather.15.cloned.1.call-done) | copy-start | bytes 9437188
  471.3 3.5 copy-start.38
  471.3 3.5 copy-start.39
  471.3 3.5 copy-start.35
  479.9 63.5 %copy-start.5 = (f32[256,1536]{1,0:T(8,128)S(1)}, f32[256,1536]{1,0:T(8,128)}, u32[]{:S(2)}) copy-start(f32[256,1536]{1,0:T(8,128)} %param.17) | copy-start | bytes 4718596
  480.0 129.4 %all-gather.23.cloned.1.call-start = ((), (), s32[]{:S(2)}) async-start(), calls=%async_computation.21 | async-start | bytes 3932160 | tf_op jit(solution)/shard_map/all_gather | solution.py:303
  542.8 0.6 copy-start.33
  545.9 182.9 %reduce-scatter.32.cloned.1.call-start = ((), (), s32[]{:S(2)}) async-start(), calls=%async_computation.29 | async-start | bytes 3538944 | tf_op jit(solution)/shard_map/reduce_scatter | solution.py:356
  553.7 177.1 %reduce-scatter.30.cloned.1.call-start = ((), (), s32[]{:S(2)}) async-start(), calls=%async_computation.28 | async-start | bytes 3538944 | tf_op jit(solution)/shard_map/reduce_scatter | solution.py:353
  561.7 194.6 %reduce-scatter.28.cloned.1.call-start = ((), (), s32[]{:S(2)}) async-start(), calls=%async_computation.27 | async-start | bytes 3538944 | tf_op jit(solution)/shard_map/reduce_scatter | solution.py:350
  569.5 39.9 %copy-start.22 = (bf16[384,1536]{0,1:T(8,128)(2,1)S(1)}, bf16[384,1536]{0,1:T(8,128)(2,1)}, u32[]{:S(2)}) copy-start(bf16[384,1536]{0,1:T(8,128)(2,1)} %all-gather.13.cloned.1.call-done) | copy-start | bytes 3538948
  569.5 224.8 %reduce-scatter.24.cloned.1.call-start = ((), (), s32[]{:S(2)}) async-start(), calls=%async_computation.25 | async-start | bytes 884736 | tf_op jit(solution)/shard_map/reduce_scatter | solution.py:344
  613.9 8.3 copy-start.3
  690.2 0.7 copy-start.19
  690.9 4.4 copy-start.12
  690.9 4.4 copy-start.14
  694.9 137.4 %reduce-scatter.22.cloned.1.call-start = ((), (), s32[]{:S(2)}) async-start(), calls=%async_computation.24 | async-start | bytes 884736 | tf_op jit(solution)/shard_map/reduce_scatter | solution.py:341
  696.6 0.7 copy-start.17
  697.4 3.9 copy-start.16
  701.3 171.4 %reduce-scatter.26.cloned.1.call-start = ((), (), s32[]{:S(2)}) async-start(), calls=%async_computation.26 | async-start | bytes 1327104 | tf_op jit(solution)/shard_map/reduce_scatter | solution.py:347
  706.1 206.9 %reduce-scatter.20.cloned.1.call-start = ((), (), s32[]{:S(2)}) async-start(), calls=%async_computation.23 | async-start | bytes 1327104 | tf_op jit(solution)/shard_map/reduce_scatter | solution.py:338
  708.8 1.9 copy-start.6
  710.7 2.9 copy-start.10
  710.7 3.0 copy-start.18
  713.6 262.1 %reduce-scatter.18.cloned.1.call-start = ((), (), s32[]{:S(2)}) async-start(), calls=%async_computation.22 | async-start | bytes 3932160 | tf_op jit(solution)/shard_map/reduce_scatter | solution.py:325
  713.7 1.3 copy-start.21
  714.9 1.9 copy-start.8
  714.9 1.9 copy-start.20
  719.7 318.9 %reduce-scatter.14.cloned.1.call-start = ((), (), s32[]{:S(2)}) async-start(), calls=%async_computation.18 | async-start | bytes 3932160 | tf_op jit(solution)/shard_map/reduce_scatter | solution.py:255
  727.9 247.7 %copy-start.1 = (f32[256,1536]{1,0:T(8,128)S(1)}, f32[256,1536]{1,0:T(8,128)}, u32[]{:S(2)}) copy-start(f32[256,1536]{1,0:T(8,128)} %param.16) | copy-start | bytes 4718596
  727.9 247.7 %copy-start.24 = (f32[1536]{0:T(1024)S(1)}, f32[1536]{0:T(1024)}, u32[]{:S(2)}) copy-start(f32[1536]{0:T(1024)} %copy-done.23) | copy-start | bytes 18436
  727.9 247.7 %copy-start.31 = (f32[256]{0:T(256)S(1)}, f32[256]{0:T(256)}, u32[]{:S(2)}) copy-start(f32[256]{0:T(256)} %copy-done.30) | copy-start | bytes 3076
  730.7 246.7 %copy-start.32 = (bf16[1536]{0:T(1024)(128)(2,1)S(1)}, bf16[1536]{0:T(1024)(128)(2,1)}, u32[]{:S(2)}) copy-start(bf16[1536]{0:T(1024)(128)(2,1)} %get-tuple-element.254) | copy-start | bytes 9220
  730.7 307.8 %copy-start.29 = (f32[256]{0:T(256)S(1)}, f32[256]{0:T(256)}, u32[]{:S(2)}) copy-start(f32[256]{0:T(256)} %copy-done.27) | copy-start | bytes 3076
  730.7 307.8 %copy-start.34 = (f32[256]{0:T(256)S(1)}, f32[256]{0:T(256)}, u32[]{:S(2)}) copy-start(f32[256]{0:T(256)} %copy-done.33) | copy-start | bytes 3076
Sparse Core Ops, SparseCore 0:
  31.4 62.7 all-gather.8
  96.1 22.5 all-gather.10
  120.6 23.9 all-gather.12
  156.9 110.7 reduce-scatter.11
  269.7 89.4 all-gather.20
  360.9 30.3 all-gather.18
  393.2 32.1 all-gather.16
  427.3 32.1 all-gather.14
  480.1 60.3 reduce-scatter.15
  546.0 63.3 all-gather.22
  612.8 44.6 reduce-scatter.31
  660.7 46.0 reduce-scatter.29
  710.2 46.0 reduce-scatter.27
  759.3 34.9 reduce-scatter.23
  797.3 34.9 reduce-scatter.21
  836.0 36.6 reduce-scatter.25
  876.3 36.6 reduce-scatter.19
  915.2 60.4 reduce-scatter.17
  978.0 60.5 reduce-scatter.13
